TPU v7x, 32 devices: a whole 2x2x4 slice. The times are simulated.
32 devices in a mesh: groups: 2 (over x), seq: 16 (over z, y, core).
Axes of the slice: x: 2, y: 2, z: 4, core: 2. Of those that a mesh axis runs over, the one named last changes fastest.
Arguments:
- query_seq: bfloat16 [8192, 6144], P(('groups', 'seq')), parts along dimension 0, may hold values from -15 to 15
- key_seq: bfloat16 [8192, 6144], P(('groups', 'seq')), parts along dimension 0, may hold values from -15 to 15
- value_seq: bfloat16 [8192, 6144], P(('groups', 'seq')), parts along dimension 0, may hold values from -288 to 288
- conv_kernel: bfloat16 [3, 4, 6144], replicated, may hold values from -3 to 3
- feature_map: bfloat16 [128, 128], replicated, may hold values from -1.5 to 1.5
- norm_gain: float32 [6144], replicated, may hold values from 0.25 to 1.75
Outputs:
- attended: bfloat16 [8192, 6144], P(('groups', 'seq')), parts along dimension 0
There are 2 independent parts, one for each index of `groups`. A program takes and returns all parts, laid end to end along the dimension named above; an argument that names none is the same for every part. Nothing has to cross between parts.
All inputs are finite; a program needn't handle non-finite values.
Results may differ from a plain program's by a relative error of at most 0.012.
The roundings to bfloat16 on the way count: a program that leaves them out, or rounds other values in their place, can miss the bound.
Values may be sent and summed in bfloat16 or wider, within the bound.
A program may use at most 128 MiB of HBM per device.

v0:
```python
import jax
import jax.numpy as jnp
from jax import lax
from jax.sharding import PartitionSpec as P

SPAN = 256


def from_behind(block, axis, distance):
    devices = range(lax.axis_size(axis))
    route = [(i - distance, i) for i in devices if i - distance in devices]
    return lax.ppermute(block, axis, route)


def short_conv(seq_rows, rim_rows, kernel):
    tap_count = kernel.shape[0]
    length = seq_rows.shape[0]
    padded = jnp.concatenate([rim_rows, seq_rows], axis=0)
    summed = jnp.zeros(seq_rows.shape, jnp.float32)
    for offset in range(tap_count):
        window = padded[tap_count - 1 - offset : tap_count - 1 - offset + length]
        summed = summed + kernel[offset].astype(jnp.float32) * window.astype(jnp.float32)
    return summed.astype(jnp.bfloat16)


def feature_rows(conv_rows, feature_map):
    head_dim = feature_map.shape[0]
    flattened = conv_rows.reshape(-1, head_dim)
    projected = jnp.dot(flattened, feature_map, preferred_element_type=jnp.float32)
    return (jax.nn.elu(projected) + 1.0).astype(jnp.bfloat16)


def block_states(key_feat, value_heads):
    block_terms = jnp.einsum(
        "cjhd,cjhe->chde", key_feat, value_heads, preferred_element_type=jnp.float32
    )
    running = jnp.cumsum(block_terms, axis=0)
    local_prefix = jnp.concatenate([jnp.zeros_like(block_terms), running[:-1]], axis=0)
    return (local_prefix, running[-1])


def on_device(query_seq, key_seq, value_seq, conv_kernel, feature_map, norm_gain):
    tok_count = query_seq.shape[0]
    model_width = query_seq.shape[1]
    head_dim = feature_map.shape[0]
    head_count = model_width // head_dim
    tap_count = conv_kernel.shape[1]
    rim_start = tok_count - (tap_count - 1)
    query_rim, key_rim, value_rim = from_behind(
        (query_seq[rim_start:], key_seq[rim_start:], value_seq[rim_start:]), "seq", 1
    )
    query_conv = short_conv(query_seq, query_rim, conv_kernel[0])
    key_conv = short_conv(key_seq, key_rim, conv_kernel[1])
    value_conv = short_conv(value_seq, value_rim, conv_kernel[2])
    block_count = tok_count // SPAN
    query_feat = feature_rows(query_conv, feature_map).reshape(
        block_count, SPAN, head_count, head_dim
    )
    key_feat = feature_rows(key_conv, feature_map).reshape(block_count, SPAN, head_count, head_dim)
    value_heads = value_conv.reshape(block_count, SPAN, head_count, head_dim)
    local_prefix, device_total = block_states(key_feat, value_heads)
    stacked = device_total.reshape(1, head_count * head_dim, head_dim)
    shares = lax.all_to_all(stacked, "seq", split_axis=1, concat_axis=0, tiled=True)
    running = jnp.cumsum(shares, axis=0)
    before = jnp.concatenate([jnp.zeros_like(shares[:1]), running[:-1]], axis=0)
    gathered = lax.all_to_all(before, "seq", split_axis=0, concat_axis=1, tiled=True)
    earlier = gathered.reshape(head_count, head_dim, head_dim)
    prefix_bf = (earlier[None] + local_prefix).astype(jnp.bfloat16)
    scores = jnp.einsum("cihd,cjhd->chij", query_feat, key_feat, preferred_element_type=jnp.float32)
    causal = lax.broadcasted_iota(jnp.int32, (SPAN, SPAN), 0) >= lax.broadcasted_iota(
        jnp.int32, (SPAN, SPAN), 1
    )
    weights = jnp.where(causal, scores, 0.0).astype(jnp.bfloat16)
    mixed_rows = jnp.einsum(
        "chij,cjhd->cihd", weights, value_heads, preferred_element_type=jnp.float32
    )
    mixed_rows = mixed_rows + jnp.einsum(
        "cihd,chde->cihe", query_feat, prefix_bf, preferred_element_type=jnp.float32
    )
    inverse_rms = lax.rsqrt(jnp.mean(mixed_rows * mixed_rows, axis=-1, keepdims=True) + 1e-06)
    normed = (mixed_rows * inverse_rms).reshape(tok_count, model_width) * norm_gain
    return normed.astype(jnp.bfloat16)


def solution(mesh):
    return jax.shard_map(
        on_device,
        mesh=mesh,
        in_specs=(
            P(("groups", "seq"), None),
            P(("groups", "seq"), None),
            P(("groups", "seq"), None),
            P(),
            P(),
            P(),
        ),
        out_specs=P(("groups", "seq"), None),
        check_vma=False,
    )
```

profile of v0, /device:TPU:18, one launch (start us, length us, event | category | flops | bytes accessed | tf_op | source)
XLA Modules:
  0.0 212.7 jit_solution(609619368015761294)
XLA Ops:
  0.0 0.9 slice.104
  0.9 1.9 collective-permute-start
  2.9 0.9 slice.120
  3.8 3.5 %collective-permute-start.2 = (bf16[3,6144]{1,0:T(4,128)(2,1)S(1)}, bf16[3,6144]{1,0:T(4,128)(2,1)S(1)}, u32[]{:S(2)}, u32[]{:S(2)}) collective-permute-start(bf16[3,6144]{1,0:T(4,128)(2,1)S(1)} %slice.120), channel_id=1, source_target_pairs={{0,1},{1,2},{2,3},{3,4},{4,5},{5,6},{6,7},{7,8},{8,9},{9,10},{10,1... | collective-permute-start | bytes 110600 | tf_op jit(solution)/shard_map/ppermute | solution.py:12
  7.3 1.4 slice_convert_fusion.7
  8.7 1.4 collective-permute-done.2
  10.1 7.4 %add_convert_fusion = bf16[256,6144]{1,0:T(8,128)(2,1)S(1)} fusion(bf16[256,6144]{1,0:T(8,128)(2,1)} %param.7, bf16[3,6144]{1,0:T(4,128)(2,1)S(1)} %collective-permute-done.2, f32[6144]{0:T(1024)S(1)} %bitcast.60, f32[6144]{0:T(1024)S(1)} %bitcast.61, f32[6144]{0:T(1024)S(1)} %bitcast.58, f32[6144]{0:T(1024)S(1)} %bitcast.59), kind=kLoop, calls=%fused_computation.17 | loop fusion | flops 33030144 | bytes 6426624 | tf_op jit(solution)/shard_map/convert_element_type | solution.py:23
  17.5 2.9 %reshape.179 = bf16[12288,128]{1,0:T(8,128)(2,1)} reshape(bf16[256,6144]{1,0:T(8,128)(2,1)S(1)} %add_convert_fusion) | data formatting | bytes 6291456 | tf_op jit(solution)/shard_map/reshape | solution.py:28
  20.4 0.0 copy-done
  20.4 6.4 %fusion.6 = bf16[12288,128]{1,0:T(8,128)(2,1)} fusion(bf16[12288,128]{1,0:T(8,128)(2,1)} %reshape.179, bf16[128,128]{1,0:T(8,128)(2,1)S(1)} %copy-done), kind=kOutput, calls=%fused_computation.11 | convolution fusion | flops 410517504 | bytes 6324224 | tf_op jit(solution)/shard_map/dot_general | solution.py:29
  26.7 3.9 %copy.21 = bf16[256,48,128]{0,2,1:T(8,128)(2,1)S(1)} copy(bf16[256,48,128]{2,1,0:T(8,128)(2,1)} %bitcast.47) | data formatting | bytes 6291456 | tf_op jit(solution)/shard_map/reshape.31
  30.6 0.0 copy-start.2
  30.6 0.0 collective-permute-done
  30.6 7.7 %fusion.21 = bf16[32,48,8,128]{3,2,1,0:T(8,128)(2,1)S(1)} fusion(bf16[256,6144]{1,0:T(8,128)(2,1)} %param.8, bf16[3,6144]{1,0:T(4,128)(2,1)S(1)} %collective-permute-done, f32[6144]{0:T(1024)S(1)} %bitcast.54, f32[6144]{0:T(1024)S(1)} %bitcast.55, f32[6144]{0:T(1024)S(1)} %bitcast.56, f32[6144]{0:T(1024)S(1)} %bitcast.57), kind=kLoop, calls=%fused_computation.40 | loop fusion | flops 33030144 | bytes 6426624
  38.4 1.0 fusion.19
  39.4 75.1 %all_to_all.21 = f32[1,6144,128]{2,0,1:T(1,128)S(1)} all-to-all(f32[1,6144,128]{2,0,1:T(1,128)S(1)} %bitcast.46), channel_id=1, replica_groups=mesh['groups'=2,'seq'=16] {'seq'}, dimensions={1} | all-to-all | bytes 6291456 | tf_op jit(solution)/shard_map/all_to_all | solution.py:63
  114.5 0.2 fusion.31
  114.8 0.1 slice.139
  114.9 1.3 concatenate.15
  116.2 4.8 %all-to-all-start.1 = ((bf16[16,384,128]{2,1,0:T(8,128)(2,1)}), bf16[16,384,128]{2,1,0:T(8,128)(2,1)}, u32[]{:S(2)}, u32[]{:S(2)}) async-start(bf16[16,384,128]{2,1,0:T(8,128)(2,1)} %concatenate.15), calls=%async_computation.1 | async-start | bytes 3145728 | tf_op jit(solution)/shard_map/all_to_all | solution.py:66
  121.0 0.9 slice.112
  122.0 2.2 %collective-permute-start.1 = (bf16[3,6144]{1,0:T(4,128)(2,1)S(1)}, bf16[3,6144]{1,0:T(4,128)(2,1)S(1)}, u32[]{:S(2)}, u32[]{:S(2)}) collective-permute-start(bf16[3,6144]{1,0:T(4,128)(2,1)S(1)} %slice.112), channel_id=1, source_target_pairs={{0,1},{1,2},{2,3},{3,4},{4,5},{5,6},{6,7},{7,8},{8,9},{9,10},{10,1... | collective-permute-start | bytes 110600 | tf_op jit(solution)/shard_map/ppermute | solution.py:12
  124.2 33.7 %collective-permute-done.1 = bf16[3,6144]{1,0:T(4,128)(2,1)S(1)} collective-permute-done((bf16[3,6144]{1,0:T(4,128)(2,1)S(1)}, bf16[3,6144]{1,0:T(4,128)(2,1)S(1)}, u32[]{:S(2)}, u32[]{:S(2)}) %collective-permute-start.1) | collective-permute-done | bytes 36896 | tf_op jit(solution)/shard_map/ppermute | solution.py:12
  157.9 7.3 %add_convert_fusion.1 = bf16[256,6144]{1,0:T(8,128)(2,1)S(1)} fusion(bf16[256,6144]{1,0:T(8,128)(2,1)} %param.6, bf16[3,6144]{1,0:T(4,128)(2,1)S(1)} %collective-permute-done.1, f32[6144]{0:T(1024)S(1)} %bitcast.51, f32[6144]{0:T(1024)S(1)} %bitcast.52, f32[6144]{0:T(1024)S(1)} %bitcast.53, f32[6144]{0:T(1024)S(1)} %bitcast.50), kind=kLoop, calls=%fused_computation.18 | loop fusion | flops 33030144 | bytes 6426624 | tf_op jit(solution)/shard_map/convert_element_type | solution.py:23
  165.2 2.9 %reshape.177 = bf16[12288,128]{1,0:T(8,128)(2,1)} reshape(bf16[256,6144]{1,0:T(8,128)(2,1)S(1)} %add_convert_fusion.1) | data formatting | bytes 6291456 | tf_op jit(solution)/shard_map/reshape | solution.py:28
  168.1 6.4 %fusion.3 = bf16[12288,128]{1,0:T(8,128)(2,1)} fusion(bf16[12288,128]{1,0:T(8,128)(2,1)} %reshape.177, bf16[128,128]{1,0:T(8,128)(2,1)S(1)} %copy-done), kind=kOutput, calls=%fused_computation.8 | convolution fusion | flops 410517504 | bytes 6324224 | tf_op jit(solution)/shard_map/dot_general | solution.py:29
  174.4 0.0 all-to-all-done.1
  174.4 6.2 %fusion.24 = f32[48,128,256]{2,1,0:T(8,128)} fusion(bf16[48,128,128]{2,1,0:T(8,128)(2,1)} %bitcast.17, bf16[256,48,128]{2,1,0:T(8,128)(2,1)} %bitcast.48), kind=kOutput, calls=%fused_computation.43 | convolution fusion | flops 402653184 | bytes 11010048 | tf_op jit(solution)/shard_map/cihd,chde->cihe/dot_general | solution.py:77
  180.7 11.1 %fusion.7 = (f32[256,48]{0,1:T(8,128)S(1)}, f32[48,128,256]{2,1,0:T(8,128)}) fusion(f32[48,128,256]{2,1,0:T(8,128)} %fusion.24, pred[256,256]{1,0:T(8,128)(4,1)S(1)} %iota_compare_fusion, bf16[256,48,128]{0,2,1:T(8,128)(2,1)S(1)} %copy-done.3, bf16[256,48,128]{2,1,0:T(8,128)(2,1)} %bitcast.49, bf16[32,48,8,128]{3,2,1,0:T(8,128)(2,1)} %copy-done.4), kind=kOutput, calls=%fused_computation.14 | convolution fusion | flops 1621610496 | bytes 22134784 | tf_op jit(solution)/shard_map/chij,cjhd->cihd/dot_general | solution.py:74
  191.8 9.3 %bitcast_multiply_fusion = f32[1,256,48,128]{1,3,2,0:T(8,128)} fusion(f32[256,48]{0,1:T(8,128)S(1)} %add_rsqrt_fusion, f32[48,128,256]{2,1,0:T(8,128)} %get-tuple-element.18, f32[48,128,256]{2,1,0:T(8,128)} %fusion.24), kind=kLoop, calls=%fused_computation.12 | loop fusion | flops 3145728 | bytes 18923520 | tf_op jit(solution)/shard_map/mul | solution.py:81
  201.1 6.6 %copy.26 = f32[256,6144]{1,0:T(8,128)} copy(f32[256,6144]{0,1:T(8,128)} %bitcast.44) | data formatting | bytes 12582912 | tf_op jit(solution)/shard_map/reshape | solution.py:81
  207.7 5.0 %multiply_convert_fusion = bf16[256,6144]{1,0:T(8,128)(2,1)} fusion(f32[256,6144]{1,0:T(8,128)} %copy.26, f32[6144]{0:T(1024)S(1)} %copy-done.5), kind=kLoop, calls=%fused_computation.15 | loop fusion | flops 3145728 | bytes 9461760 | tf_op jit(solution)/shard_map/convert_element_type | solution.py:82
  (12 shorter events, 0.1 us)
Async XLA Ops:
  0.0 20.4 %copy-start = (bf16[128,128]{1,0:T(8,128)(2,1)S(1)}, bf16[128,128]{1,0:T(8,128)(2,1)}, u32[]{:S(2)}) copy-start(bf16[128,128]{1,0:T(8,128)(2,1)} %param.10) | copy-start | bytes 98308
  0.9 29.7 %collective-permute-start = (bf16[3,6144]{1,0:T(4,128)(2,1)S(1)}, bf16[3,6144]{1,0:T(4,128)(2,1)S(1)}, u32[]{:S(2)}, u32[]{:S(2)}) collective-permute-start(bf16[3,6144]{1,0:T(4,128)(2,1)S(1)} %slice.104), channel_id=1, source_target_pairs={{0,1},{1,2},{2,3},{3,4},{4,5},{5,6},{6,7},{7,8},{8,9},{9,10},{10,1... | collective-permute-start | bytes 110600 | tf_op jit(solution)/shard_map/ppermute | solution.py:12
  3.8 6.3 %collective-permute-start.2 = (bf16[3,6144]{1,0:T(4,128)(2,1)S(1)}, bf16[3,6144]{1,0:T(4,128)(2,1)S(1)}, u32[]{:S(2)}, u32[]{:S(2)}) collective-permute-start(bf16[3,6144]{1,0:T(4,128)(2,1)S(1)} %slice.120), channel_id=1, source_target_pairs={{0,1},{1,2},{2,3},{3,4},{4,5},{5,6},{6,7},{7,8},{8,9},{9,10},{10,1... | collective-permute-start | bytes 110600 | tf_op jit(solution)/shard_map/ppermute | solution.py:12
  30.6 8.8 %copy-start.2 = (bf16[256,48,128]{0,2,1:T(8,128)(2,1)}, bf16[256,48,128]{0,2,1:T(8,128)(2,1)S(1)}, u32[]{:S(2)}) copy-start(bf16[256,48,128]{0,2,1:T(8,128)(2,1)S(1)} %copy.21) | copy-start | bytes 9437188
  38.4 76.2 %copy-start.4 = (bf16[32,48,8,128]{3,2,1,0:T(8,128)(2,1)}, bf16[32,48,8,128]{3,2,1,0:T(8,128)(2,1)S(1)}, u32[]{:S(2)}) copy-start(bf16[32,48,8,128]{3,2,1,0:T(8,128)(2,1)S(1)} %fusion.21) | copy-start | bytes 9437188
  116.2 58.2 %all-to-all-start.1 = ((bf16[16,384,128]{2,1,0:T(8,128)(2,1)}), bf16[16,384,128]{2,1,0:T(8,128)(2,1)}, u32[]{:S(2)}, u32[]{:S(2)}) async-start(bf16[16,384,128]{2,1,0:T(8,128)(2,1)} %concatenate.15), calls=%async_computation.1 | async-start | bytes 3145728 | tf_op jit(solution)/shard_map/all_to_all | solution.py:66
  122.0 35.9 %collective-permute-start.1 = (bf16[3,6144]{1,0:T(4,128)(2,1)S(1)}, bf16[3,6144]{1,0:T(4,128)(2,1)S(1)}, u32[]{:S(2)}, u32[]{:S(2)}) collective-permute-start(bf16[3,6144]{1,0:T(4,128)(2,1)S(1)} %slice.112), channel_id=1, source_target_pairs={{0,1},{1,2},{2,3},{3,4},{4,5},{5,6},{6,7},{7,8},{8,9},{9,10},{10,1... | collective-permute-start | bytes 110600 | tf_op jit(solution)/shard_map/ppermute | solution.py:12
  174.4 6.2 %copy-start.3 = (bf16[256,48,128]{0,2,1:T(8,128)(2,1)S(1)}, bf16[256,48,128]{0,2,1:T(8,128)(2,1)}, u32[]{:S(2)}) copy-start(bf16[256,48,128]{0,2,1:T(8,128)(2,1)} %copy-done.2) | copy-start | bytes 9437188
  201.1 6.6 %copy-start.5 = (f32[6144]{0:T(1024)S(1)}, f32[6144]{0:T(1024)}, u32[]{:S(2)}) copy-start(f32[6144]{0:T(1024)} %param.11) | copy-start | bytes 73732
  201.1 11.6 %copy-start.1 = (bf16[128,128]{1,0:T(8,128)(2,1)S(1)}, bf16[128,128]{1,0:T(8,128)(2,1)}, u32[]{:S(2)}) copy-start(bf16[128,128]{1,0:T(8,128)(2,1)} %param.10) | copy-start | bytes 98308
where the time goes:
time: 213 us
  blocking collectives  75.1 us (35%)
  other arithmetic  38.3 us (18%)
  waiting for transfers between devices  35.1 us (16%)
  matrix products  31.1 us (15%)
  local copies, waits for them, and re-layouts  20.5 us (10%)
  starting transfers between devices  12.5 us (6%)
    all_to_all x1, blocking collectives, on_device(): lax.all_to_all(stacked, 'seq', split_axis=1, concat_axis=0, tiled=True)  75.1 us
    ppermute x3, waiting for transfers between devices, from_behind(): return lax.ppermute(block, axis, route)  35.1 us
    convert_element_type x2, other arithmetic, short_conv(): return summed.astype(jnp.bfloat16)  14.7 us
    dot_general x2, matrix products, feature_rows(): jnp.dot(flattened, feature_map, preferred_element_type=jnp.float32)  12.7 us
    dot_general x1, matrix products, on_device(): jnp.einsum('chij,cjhd->cihd', weights, value_heads, preferred_element_typ...  11.1 us
    mul x1, other arithmetic, on_device(): mixed_rows * inverse_rms  9.28 us
    unnamed x1, other arithmetic  7.72 us
    ppermute x3, starting transfers between devices, from_behind(): return lax.ppermute(block, axis, route)  7.66 us
  transfers between devices with their start and end apart: 4, of which 2 were waited for; matrix products, arithmetic and copies ran while one was open for 19% of the time, Pallas kernels for 0%

commit v1 on v0

v1 whole, which is shorter than its diff:
```python
import functools

import jax
import jax.numpy as jnp
from jax import lax
from jax.experimental import pallas as pl
from jax.experimental.pallas import tpu as pltpu
from jax.sharding import PartitionSpec as P

MESH = pl.DeviceIdType.MESH
F32 = jnp.float32
BF16 = jnp.bfloat16
RIM = 8
ROWS = 64
Z_LAG = 2
Y_LAG = 2
P_LAG = 1
Q_LAG = 3


def short_conv(buf, rim, taps, which, col, width):
    tap_rows = taps[which, :, pl.ds(col, width)].astype(F32)
    tap_count = tap_rows.shape[0]
    length = buf.shape[0]
    above = rim[:, pl.ds(col, width)].astype(F32)
    out = []
    for start in range(0, length, ROWS):
        rows = buf[start : start + ROWS, pl.ds(col, width)].astype(F32)
        padded = jnp.concatenate([above, rows], axis=0)
        total = tap_rows[0:1] * rows
        for offset in range(1, tap_count):
            window = padded[RIM - offset : RIM - offset + ROWS]
            total = total + tap_rows[offset : offset + 1] * window
        out.append(total.astype(BF16))
        above = rows[ROWS - RIM :]
    return jnp.concatenate(out, axis=0)


def features(conv_rows, wide_map):
    projected = jnp.dot(conv_rows, wide_map[...], preferred_element_type=F32)
    return jnp.where(projected > 0, projected + 1.0, jnp.exp(projected)).astype(BF16)


def kernel(
    devices,
    q_hbm,
    k_hbm,
    v_hbm,
    taps,
    feature_map,
    gain,
    out_hbm,
    q_buf,
    k_buf,
    v_buf,
    q_rim,
    k_rim,
    v_rim,
    wide_map,
    q_feat,
    k_feat,
    v_conv,
    mixed,
    out_buf,
    own_state,
    x_out,
    x_in,
    z_out,
    z_in,
    y_out,
    y_in,
    p_out,
    prefix,
    load_sem,
    store_sem,
    rim_sem,
    x_sem,
    z_sem,
    y_sem,
    p_sem,
):
    tokens, width = q_buf.shape
    dim = feature_map.shape[0]
    pair = 2 * dim
    chunk = 2 * pair
    chunks = width // chunk
    me = lax.axis_index("seq")
    core = lax.rem(me, 2)
    y = lax.rem(me // 2, 2)
    z = me // 4
    planes = devices // 4
    partner = me + 1 - 2 * core
    across = me + 2 - 4 * y

    def load(hbm, buf, which, c):
        cols = pl.ds(pl.multiple_of(c * chunk, chunk), chunk)
        return pltpu.make_async_copy(hbm.at[:, cols], buf.at[:, cols], load_sem.at[which, c])

    @pl.loop(0, chunks)
    def _(c):
        load(k_hbm, k_buf, 1, c).start()
        load(v_hbm, v_buf, 2, c).start()

    barrier = pltpu.get_barrier_semaphore()

    def greet(target):
        pl.semaphore_signal(barrier, inc=1, device_id={"seq": target}, device_id_type=MESH)

    greet(partner)
    greet(across)

    @pl.when(me > 0)
    def _():
        greet(me - 1)

    @pl.when(me < devices - 1)
    def _():
        greet(me + 1)

    @pl.when(z > 0)
    def _():
        greet(me - 4)

    @pl.when(z < planes - 1)
    def _():
        greet(me + 4)

    @pl.loop(0, chunks)
    def _(c):
        load(q_hbm, q_buf, 0, c).start()

    wide_map[...] = jnp.zeros_like(wide_map)
    wide_map[:dim, :dim] = feature_map[...]
    wide_map[dim:, dim:] = feature_map[...]

    @pl.when(me == 0)
    def _():
        q_rim[...] = jnp.zeros_like(q_rim)
        k_rim[...] = jnp.zeros_like(k_rim)
        v_rim[...] = jnp.zeros_like(v_rim)

    @pl.when(z == 0)
    def _():
        @pl.loop(0, chunks)
        def _(c):
            z_in[c] = jnp.zeros(z_in.shape[1:], BF16)

    edges = [(me > 0), (me < devices - 1), (z > 0), (z < planes - 1)]
    pl.semaphore_wait(barrier, 2 + sum(e.astype(jnp.int32) for e in edges))

    def rim_copy(hbm, rim, which):
        return pltpu.make_async_remote_copy(
            src_ref=hbm.at[pl.ds(tokens - RIM, RIM)],
            dst_ref=rim,
            send_sem=rim_sem.at[0, which],
            recv_sem=rim_sem.at[1, which],
            device_id={"seq": lax.rem(me + 1, devices)},
            device_id_type=MESH,
        )

    rims = [
        rim_copy(k_hbm, k_rim, 1),
        rim_copy(v_hbm, v_rim, 2),
        rim_copy(q_hbm, q_rim, 0),
    ]

    @pl.when(me < devices - 1)
    def _():
        for copy in rims:
            copy.start()

    @pl.when(me > 0)
    def _():
        for copy in rims[:2]:
            copy.wait_recv()

    def send(src, dst, sem, c, target):
        return pltpu.make_async_remote_copy(
            src_ref=src,
            dst_ref=dst,
            send_sem=sem.at[0, c],
            recv_sem=sem.at[1, c],
            device_id={"seq": target},
            device_id_type=MESH,
        )

    def x_copy(c):
        return send(x_out.at[c], x_in.at[c], x_sem, c, partner)

    def z_copy(c):
        return send(z_out.at[c], z_in.at[c], z_sem, c, lax.rem(me + 4, devices))

    def y_copy(c):
        return send(y_out.at[c], y_in.at[c], y_sem, c, across)

    def p_copy(c):
        return send(p_out.at[c], prefix.at[c, core], p_sem, c, partner)

    def pair_state(col):
        k_rows = short_conv(k_buf, k_rim, taps, 1, col, pair)
        v_rows = short_conv(v_buf, v_rim, taps, 2, col, pair)
        feat = features(k_rows, wide_map)
        k_feat[:, pl.ds(col, pair)] = feat
        v_conv[:, pl.ds(col, pair)] = v_rows
        both = lax.dot_general(feat, v_rows, (((0,), (0,)), ((), ())), preferred_element_type=F32)
        return both[:dim, :dim], both[dim:, dim:]

    def states(c):
        load(k_hbm, k_buf, 1, c).wait()
        load(v_hbm, v_buf, 2, c).wait()
        for mine in (False, True):
            side = core if mine else 1 - core
            col = pl.multiple_of(c * chunk + side * pair, pair)
            first, second = pair_state(col)
            if mine:
                own_state[c, :dim] = first
                own_state[c, dim:] = second
            else:
                x_out[c, :dim] = first.astype(BF16)
                x_out[c, dim:] = second.astype(BF16)
                x_copy(c).start()

    def relay_z(c):
        x_copy(c).wait_recv()

        @pl.when(z > 0)
        def _():
            z_copy(c).wait_recv()

        before = z_in[c].astype(F32)
        chip = own_state[c] + x_in[c].astype(F32)
        z_out[c] = (before + chip).astype(BF16)

        @pl.when(z < planes - 1)
        def _():
            z_copy(c).start()

        y_out[c] = (before + jnp.where(y == 0, chip, 0.0)).astype(BF16)
        y_copy(c).start()

    def relay_y(c):
        y_copy(c).wait_recv()
        earlier = z_in[c].astype(F32) + y_in[c].astype(F32)
        p_out[c] = (earlier + jnp.where(core == 0, own_state[c], 0.0)).astype(BF16)
        p_copy(c).start()
        prefix[c, core] = (earlier + jnp.where(core == 1, x_in[c].astype(F32), 0.0)).astype(BF16)

    def local_mix(c):
        load(q_hbm, q_buf, 0, c).wait()
        row = lax.broadcasted_iota(jnp.int32, (tokens, tokens), 0)
        causal = row >= lax.broadcasted_iota(jnp.int32, (tokens, tokens), 1)
        for side in range(2):
            col = pl.multiple_of(c * chunk + side * pair, pair)
            q_rows = short_conv(q_buf, q_rim, taps, 0, col, pair)
            feat = features(q_rows, wide_map)
            q_feat[:, pl.ds(col, pair)] = feat
            for head in range(2):
                cols = pl.ds(pl.multiple_of(col + head * dim, dim), dim)
                scores = lax.dot_general(
                    feat[:, head * dim : (head + 1) * dim],
                    k_feat[:, cols],
                    (((1,), (1,)), ((), ())),
                    preferred_element_type=F32,
                )
                weights = jnp.where(causal, scores, 0.0).astype(BF16)
                mixed[:, cols] = jnp.dot(weights, v_conv[:, cols], preferred_element_type=F32)

    def store(c):
        cols = pl.ds(pl.multiple_of(c * chunk, chunk), chunk)
        return pltpu.make_async_copy(out_buf.at[:, cols], out_hbm.at[:, cols], store_sem.at[c])

    def finish(c):
        p_copy(c).wait_recv()
        for head in range(4):
            cols = pl.ds(pl.multiple_of(c * chunk + head * dim, dim), dim)
            state = prefix[c, head // 2, (head % 2) * dim : (head % 2 + 1) * dim]
            rows = mixed[:, cols] + jnp.dot(q_feat[:, cols], state, preferred_element_type=F32)
            scale = lax.rsqrt(jnp.mean(rows * rows, axis=-1, keepdims=True) + 1e-06)
            out_buf[:, cols] = (rows * scale * gain[:, cols]).astype(BF16)
        store(c).start()

    z_lag = 1 + Z_LAG * z
    y_lag = z_lag + Y_LAG
    last_lag = jnp.maximum(y_lag + P_LAG, Q_LAG)

    def at(step, lag, work):
        c = step - lag

        @pl.when((c >= 0) & (c < chunks))
        def _():
            work(c)

    @pl.loop(0, chunks + last_lag)
    def _(step):
        at(step, 0, states)
        at(step, z_lag, relay_z)
        at(step, y_lag, relay_y)

        @pl.when((me > 0) & (step == Q_LAG))
        def _():
            rims[2].wait_recv()

        at(step, Q_LAG, local_mix)
        at(step, last_lag, finish)

    @pl.when(me < devices - 1)
    def _():
        for copy in rims:
            copy.wait_send()

    @pl.loop(0, chunks)
    def _(c):
        x_copy(c).wait_send()

        @pl.when(z < planes - 1)
        def _():
            z_copy(c).wait_send()

        y_copy(c).wait_send()
        p_copy(c).wait_send()
        store(c).wait()


def on_device(query_seq, key_seq, value_seq, conv_kernel, feature_map, norm_gain):
    tokens, width = query_seq.shape
    dim = feature_map.shape[0]
    devices = lax.axis_size("seq")
    chunks = width // (4 * dim)
    rows = pltpu.VMEM((tokens, width), BF16)
    rim = pltpu.VMEM((RIM, width), BF16)
    slots = pltpu.VMEM((chunks, 2 * dim, dim), BF16)
    ways = pltpu.SemaphoreType.DMA((2, chunks))
    hbm = pl.BlockSpec(memory_space=pl.ANY)
    vmem = pl.BlockSpec(memory_space=pltpu.VMEM)
    return pl.pallas_call(
        functools.partial(kernel, devices),
        out_shape=jax.ShapeDtypeStruct((tokens, width), BF16),
        in_specs=[hbm, hbm, hbm, vmem, vmem, vmem],
        out_specs=hbm,
        scratch_shapes=[
            rows,
            rows,
            rows,
            rim,
            rim,
            rim,
            pltpu.VMEM((2 * dim, 2 * dim), BF16),
            rows,
            rows,
            rows,
            pltpu.VMEM((tokens, width), F32),
            rows,
            pltpu.VMEM((chunks, 2 * dim, dim), F32),
            slots,
            slots,
            slots,
            slots,
            slots,
            slots,
            slots,
            pltpu.VMEM((chunks, 2, 2 * dim, dim), BF16),
            pltpu.SemaphoreType.DMA((3, chunks)),
            pltpu.SemaphoreType.DMA((chunks,)),
            pltpu.SemaphoreType.DMA((2, 3)),
            ways,
            ways,
            ways,
            ways,
        ],
        compiler_params=pltpu.CompilerParams(
            collective_id=0, has_side_effects=True, vmem_limit_bytes=60 * 1024 * 1024
        ),
        name="layer",
    )(query_seq, key_seq, value_seq, conv_kernel, feature_map, norm_gain.reshape(1, width))


def solution(mesh):
    split = P(("groups", "seq"), None)
    return jax.shard_map(
        on_device,
        mesh=mesh,
        in_specs=(split, split, split, P(), P(), P()),
        out_specs=split,
        check_vma=False,
    )
```

time: 213 us -> 52.9 us (0.25)
  the two profiles are of different devices: /device:TPU:18 before, /device:TPU:29 now
where the time goes in v1:
time: 52.9 us; the launch traced here: 52.7 us
  Pallas kernels  48.8 us (92%)
  local copies, waits for them, and re-layouts  3.88 us (7%)
    pallas_call x1, Pallas kernels, on_device(): pl.pallas_call(functools.partial(kernel, devices), out_shape=jax.ShapeDty...  48.8 us
    unnamed x1, local copies, waits for them, and re-layouts  3.88 us

profile of v1, /device:TPU:29, one launch (start us, length us, event | category | flops | bytes accessed | tf_op | source)
XLA Modules:
  0.0 52.7 jit_solution(13429802585658085938)
XLA Ops:
  0.0 48.8 %layer.1 = bf16[256,6144]{1,0:T(8,128)(2,1)} custom-call(bf16[256,6144]{1,0:T(8,128)(2,1)} %q_hbm.1, bf16[256,6144]{1,0:T(8,128)(2,1)} %k_hbm.1, bf16[256,6144]{1,0:T(8,128)(2,1)} %v_hbm.1, bf16[3,4,6144]{2,1,0:T(4,128)(2,1)} %taps.1, bf16[128,128]{1,0:T(8,128)(2,1)} %feature_map.1, f32[1,6144]{1,0:T(1,128)} %bitcast.1), custom_call_target="tpu_custom_call" | custom-call | tf_op jit(solution)/shard_map/layer/pallas_call | solution.py:335
  48.8 3.9 %copy.8 = bf16[256,6144]{1,0:T(8,128)(2,1)} copy(bf16[256,6144]{1,0:T(8,128)(2,1)} %layer.1) | data formatting | bytes 6291456

commit v2 on v1

--- a/solution.py
+++ b/solution.py
@@ -13,9 +13,10 @@
 RIM = 8
 ROWS = 64
 Z_LAG = 2
-Y_LAG = 2
-P_LAG = 1
-Q_LAG = 3
+Y_LAG = 3
+P_LAG = 2
+Q_FIRST = 12
+Q_SLOPE = 3
 
 
 def short_conv(buf, rim, taps, which, col, width):
@@ -49,7 +50,7 @@
     taps,
     feature_map,
     gain,
-    out_hbm,
+    out_buf,
     q_buf,
     k_buf,
     v_buf,
@@ -61,7 +62,6 @@
     k_feat,
     v_conv,
     mixed,
-    out_buf,
     own_state,
     x_out,
     x_in,
@@ -72,7 +72,6 @@
     p_out,
     prefix,
     load_sem,
-    store_sem,
     rim_sem,
     x_sem,
     z_sem,
@@ -148,53 +147,51 @@
     edges = [(me > 0), (me < devices - 1), (z > 0), (z < planes - 1)]
     pl.semaphore_wait(barrier, 2 + sum(e.astype(jnp.int32) for e in edges))
 
-    def rim_copy(hbm, rim, which):
+    def rim_copy(which, c):
+        hbm, rim = ((q_hbm, q_rim), (k_hbm, k_rim), (v_hbm, v_rim))[which]
+        cols = pl.ds(pl.multiple_of(c * chunk, chunk), chunk)
         return pltpu.make_async_remote_copy(
-            src_ref=hbm.at[pl.ds(tokens - RIM, RIM)],
-            dst_ref=rim,
-            send_sem=rim_sem.at[0, which],
-            recv_sem=rim_sem.at[1, which],
+            src_ref=hbm.at[pl.ds(tokens - RIM, RIM), cols],
+            dst_ref=rim.at[:, cols],
+            send_sem=rim_sem.at[0, which, c],
+            recv_sem=rim_sem.at[1, which, c],
             device_id={"seq": lax.rem(me + 1, devices)},
             device_id_type=MESH,
         )
 
-    rims = [
-        rim_copy(k_hbm, k_rim, 1),
-        rim_copy(v_hbm, v_rim, 2),
-        rim_copy(q_hbm, q_rim, 0),
-    ]
-
     @pl.when(me < devices - 1)
     def _():
-        for copy in rims:
-            copy.start()
-
-    @pl.when(me > 0)
-    def _():
-        for copy in rims[:2]:
-            copy.wait_recv()
-
-    def send(src, dst, sem, c, target):
+        @pl.loop(0, chunks)
+        def _(c):
+            rim_copy(1, c).start()
+            rim_copy(2, c).start()
+
+        @pl.loop(0, chunks)
+        def _(c):
+            rim_copy(0, c).start()
+
+    def send(src, dst, sem, c, h, target):
+        rows = pl.ds(h * dim, dim)
         return pltpu.make_async_remote_copy(
-            src_ref=src,
-            dst_ref=dst,
-            send_sem=sem.at[0, c],
-            recv_sem=sem.at[1, c],
+            src_ref=src.at[rows],
+            dst_ref=dst.at[rows],
+            send_sem=sem.at[0, c, h],
+            recv_sem=sem.at[1, c, h],
             device_id={"seq": target},
             device_id_type=MESH,
         )
 
-    def x_copy(c):
-        return send(x_out.at[c], x_in.at[c], x_sem, c, partner)
-
-    def z_copy(c):
-        return send(z_out.at[c], z_in.at[c], z_sem, c, lax.rem(me + 4, devices))
-
-    def y_copy(c):
-        return send(y_out.at[c], y_in.at[c], y_sem, c, across)
-
-    def p_copy(c):
-        return send(p_out.at[c], prefix.at[c, core], p_sem, c, partner)
+    def x_copy(c, h):
+        return send(x_out.at[c], x_in.at[c], x_sem, c, h, partner)
+
+    def z_copy(c, h):
+        return send(z_out.at[c], z_in.at[c], z_sem, c, h, lax.rem(me + 4, devices))
+
+    def y_copy(c, h):
+        return send(y_out.at[c], y_in.at[c], y_sem, c, h, across)
+
+    def p_copy(c, h):
+        return send(p_out.at[c], prefix.at[c, core], p_sem, c, h, partner)
 
     def pair_state(col):
         k_rows = short_conv(k_buf, k_rim, taps, 1, col, pair)
@@ -208,6 +205,12 @@
     def states(c):
         load(k_hbm, k_buf, 1, c).wait()
         load(v_hbm, v_buf, 2, c).wait()
+
+        @pl.when(me > 0)
+        def _():
+            rim_copy(1, c).wait_recv()
+            rim_copy(2, c).wait_recv()
+
         for mine in (False, True):
             side = core if mine else 1 - core
             col = pl.multiple_of(c * chunk + side * pair, pair)
@@ -218,35 +221,47 @@
             else:
                 x_out[c, :dim] = first.astype(BF16)
                 x_out[c, dim:] = second.astype(BF16)
-                x_copy(c).start()
+
+        x_copy(c, 0).start()
+        x_copy(c, 1).start()
 
     def relay_z(c):
-        x_copy(c).wait_recv()
-
-        @pl.when(z > 0)
-        def _():
-            z_copy(c).wait_recv()
-
-        before = z_in[c].astype(F32)
-        chip = own_state[c] + x_in[c].astype(F32)
-        z_out[c] = (before + chip).astype(BF16)
-
-        @pl.when(z < planes - 1)
-        def _():
-            z_copy(c).start()
-
-        y_out[c] = (before + jnp.where(y == 0, chip, 0.0)).astype(BF16)
-        y_copy(c).start()
+        for h in range(2):
+            rows = pl.ds(h * dim, dim)
+            x_copy(c, h).wait_recv()
+
+            @pl.when(z > 0)
+            def _():
+                z_copy(c, h).wait_recv()
+
+            before = z_in[c, rows].astype(F32)
+            chip = own_state[c, rows] + x_in[c, rows].astype(F32)
+            z_out[c, rows] = (before + chip).astype(BF16)
+
+            @pl.when(z < planes - 1)
+            def _():
+                z_copy(c, h).start()
+
+            y_out[c, rows] = (before + jnp.where(y == 0, chip, 0.0)).astype(BF16)
+            y_copy(c, h).start()
 
     def relay_y(c):
-        y_copy(c).wait_recv()
-        earlier = z_in[c].astype(F32) + y_in[c].astype(F32)
-        p_out[c] = (earlier + jnp.where(core == 0, own_state[c], 0.0)).astype(BF16)
-        p_copy(c).start()
-        prefix[c, core] = (earlier + jnp.where(core == 1, x_in[c].astype(F32), 0.0)).astype(BF16)
+        for h in range(2):
+            rows = pl.ds(h * dim, dim)
+            y_copy(c, h).wait_recv()
+            earlier = z_in[c, rows].astype(F32) + y_in[c, rows].astype(F32)
+            p_out[c, rows] = (earlier + jnp.where(core == 0, own_state[c, rows], 0.0)).astype(BF16)
+            p_copy(c, h).start()
+            own = earlier + jnp.where(core == 1, x_in[c, rows].astype(F32), 0.0)
+            prefix[c, core, rows] = own.astype(BF16)
 
     def local_mix(c):
         load(q_hbm, q_buf, 0, c).wait()
+
+        @pl.when(me > 0)
+        def _():
+            rim_copy(0, c).wait_recv()
+
         row = lax.broadcasted_iota(jnp.int32, (tokens, tokens), 0)
         causal = row >= lax.broadcasted_iota(jnp.int32, (tokens, tokens), 1)
         for side in range(2):
@@ -265,23 +280,20 @@
                 weights = jnp.where(causal, scores, 0.0).astype(BF16)
                 mixed[:, cols] = jnp.dot(weights, v_conv[:, cols], preferred_element_type=F32)
 
-    def store(c):
-        cols = pl.ds(pl.multiple_of(c * chunk, chunk), chunk)
-        return pltpu.make_async_copy(out_buf.at[:, cols], out_hbm.at[:, cols], store_sem.at[c])
-
     def finish(c):
-        p_copy(c).wait_recv()
+        p_copy(c, 0).wait_recv()
+        p_copy(c, 1).wait_recv()
         for head in range(4):
             cols = pl.ds(pl.multiple_of(c * chunk + head * dim, dim), dim)
             state = prefix[c, head // 2, (head % 2) * dim : (head % 2 + 1) * dim]
             rows = mixed[:, cols] + jnp.dot(q_feat[:, cols], state, preferred_element_type=F32)
             scale = lax.rsqrt(jnp.mean(rows * rows, axis=-1, keepdims=True) + 1e-06)
             out_buf[:, cols] = (rows * scale * gain[:, cols]).astype(BF16)
-        store(c).start()
 
     z_lag = 1 + Z_LAG * z
     y_lag = z_lag + Y_LAG
-    last_lag = jnp.maximum(y_lag + P_LAG, Q_LAG)
+    q_lag = jnp.maximum(Q_FIRST - Q_SLOPE * z, 1)
+    last_lag = jnp.maximum(y_lag + P_LAG, q_lag)
 
     def at(step, lag, work):
         c = step - lag
@@ -296,29 +308,29 @@
         at(step, z_lag, relay_z)
         at(step, y_lag, relay_y)
 
-        @pl.when((me > 0) & (step == Q_LAG))
-        def _():
-            rims[2].wait_recv()
-
-        at(step, Q_LAG, local_mix)
+        at(step, q_lag, local_mix)
         at(step, last_lag, finish)
 
     @pl.when(me < devices - 1)
     def _():
-        for copy in rims:
-            copy.wait_send()
+        @pl.loop(0, chunks)
+        def _(c):
+            for which in range(3):
+                rim_copy(which, c).wait_send()
 
     @pl.loop(0, chunks)
     def _(c):
-        x_copy(c).wait_send()
-
-        @pl.when(z < planes - 1)
-        def _():
-            z_copy(c).wait_send()
-
-        y_copy(c).wait_send()
-        p_copy(c).wait_send()
-        store(c).wait()
+        for h in range(2):
+            x_copy(c, h).wait_send()
+            y_copy(c, h).wait_send()
+            p_copy(c, h).wait_send()
+
+    @pl.when(z < planes - 1)
+    def _():
+        @pl.loop(0, chunks)
+        def _(c):
+            for h in range(2):
+                z_copy(c, h).wait_send()
 
 
 def on_device(query_seq, key_seq, value_seq, conv_kernel, feature_map, norm_gain):
@@ -329,14 +341,14 @@
     rows = pltpu.VMEM((tokens, width), BF16)
     rim = pltpu.VMEM((RIM, width), BF16)
     slots = pltpu.VMEM((chunks, 2 * dim, dim), BF16)
-    ways = pltpu.SemaphoreType.DMA((2, chunks))
+    ways = pltpu.SemaphoreType.DMA((2, chunks, 2))
     hbm = pl.BlockSpec(memory_space=pl.ANY)
     vmem = pl.BlockSpec(memory_space=pltpu.VMEM)
     return pl.pallas_call(
         functools.partial(kernel, devices),
-        out_shape=jax.ShapeDtypeStruct((tokens, width), BF16),
+        out_shape=pltpu.MemorySpace.VMEM((tokens, width), BF16),
         in_specs=[hbm, hbm, hbm, vmem, vmem, vmem],
-        out_specs=hbm,
+        out_specs=vmem,
         scratch_shapes=[
             rows,
             rows,
@@ -349,7 +361,6 @@
             rows,
             rows,
             pltpu.VMEM((tokens, width), F32),
-            rows,
             pltpu.VMEM((chunks, 2 * dim, dim), F32),
             slots,
             slots,
@@ -360,8 +371,7 @@
             slots,
             pltpu.VMEM((chunks, 2, 2 * dim, dim), BF16),
             pltpu.SemaphoreType.DMA((3, chunks)),
-            pltpu.SemaphoreType.DMA((chunks,)),
-            pltpu.SemaphoreType.DMA((2, 3)),
+            pltpu.SemaphoreType.DMA((2, 3, chunks)),
             ways,
             ways,
             ways,

time: 52.9 us -> 43.8 us (0.83)
  the two profiles are of different devices: /device:TPU:29 before, /device:TPU:0 now
where the time goes in v2:
time: 43.8 us; the launch traced here: 43.7 us
  Pallas kernels  42 us (96%)
  local copies, waits for them, and re-layouts  1.67 us (4%)
    pallas_call x1, Pallas kernels, on_device(): pl.pallas_call(functools.partial(kernel, devices), out_shape=pltpu.Memory...  42 us
    unnamed x1, local copies, waits for them, and re-layouts  1.67 us

profile of v2, /device:TPU:0, one launch (start us, length us, event | category | flops | bytes accessed | tf_op | source)
XLA Modules:
  0.0 43.7 jit_solution(13879121792259043321)
XLA Ops:
  0.0 42.0 %layer.1 = bf16[256,6144]{1,0:T(8,128)(2,1)S(1)} custom-call(bf16[256,6144]{1,0:T(8,128)(2,1)} %q_hbm.1, bf16[256,6144]{1,0:T(8,128)(2,1)} %k_hbm.1, bf16[256,6144]{1,0:T(8,128)(2,1)} %v_hbm.1, bf16[3,4,6144]{2,1,0:T(4,128)(2,1)} %taps.1, bf16[128,128]{1,0:T(8,128)(2,1)} %feature_map.1, f32[1,6144]{1,0:T(1,128)} %bitcast.1), custom_call_target="tpu_custom_call" | custom-call | tf_op jit(solution)/shard_map/layer/pallas_call | solution.py:347
  42.0 1.7 %copy.8 = bf16[256,6144]{1,0:T(8,128)(2,1)} copy(bf16[256,6144]{1,0:T(8,128)(2,1)S(1)} %layer.1) | data formatting | bytes 6291456

commit v3 on v2

--- a/solution.py
+++ b/solution.py
@@ -306,9 +306,8 @@
     def _(step):
         at(step, 0, states)
         at(step, z_lag, relay_z)
+        at(step, q_lag, local_mix)
         at(step, y_lag, relay_y)
-
-        at(step, q_lag, local_mix)
         at(step, last_lag, finish)
 
     @pl.when(me < devices - 1)

time: 43.8 us -> 42.9 us (0.979)
  Pallas kernels: 42 us -> 41.1 us
    pallas_call x1, Pallas kernels: 42 us -> 41.1 us  [on_device(): pl.pallas_call(functools.partial(kernel, devices), out_shape=pltpu.Memory...]
where the time goes in v3:
time: 42.9 us; the launch traced here: 42.8 us
  Pallas kernels  41.1 us (96%)
  local copies, waits for them, and re-layouts  1.67 us (4%)
    pallas_call x1, Pallas kernels, on_device(): pl.pallas_call(functools.partial(kernel, devices), out_shape=pltpu.Memory...  41.1 us
    unnamed x1, local copies, waits for them, and re-layouts  1.67 us

profile of v3, /device:TPU:0, one launch (start us, length us, event | category | flops | bytes accessed | tf_op | source)
XLA Modules:
  0.0 42.8 jit_solution(3488612260619939279)
XLA Ops:
  0.0 41.1 %layer.1 = bf16[256,6144]{1,0:T(8,128)(2,1)S(1)} custom-call(bf16[256,6144]{1,0:T(8,128)(2,1)} %q_hbm.1, bf16[256,6144]{1,0:T(8,128)(2,1)} %k_hbm.1, bf16[256,6144]{1,0:T(8,128)(2,1)} %v_hbm.1, bf16[3,4,6144]{2,1,0:T(4,128)(2,1)} %taps.1, bf16[128,128]{1,0:T(8,128)(2,1)} %feature_map.1, f32[1,6144]{1,0:T(1,128)} %bitcast.1), custom_call_target="tpu_custom_call" | custom-call | tf_op jit(solution)/shard_map/layer/pallas_call | solution.py:346
  41.1 1.7 %copy.8 = bf16[256,6144]{1,0:T(8,128)(2,1)} copy(bf16[256,6144]{1,0:T(8,128)(2,1)S(1)} %layer.1) | data formatting | bytes 6291456
